TPU v7x, 32 devices: a whole 2x2x4 slice. The times are simulated.
32 devices in a mesh: feed: 8 (over y, x, core), tm: 4 (over z).
Axes of the slice: x: 2, y: 2, z: 4, core: 2. Of those that a mesh axis runs over, the one named last changes fastest.
Arguments:
- voltages: bfloat16 [256, 1048576], P('feed', 'tm'), may hold values from -12 to 12
- filter_taps: float32 [4, 1024], replicated, may hold values from -1 to 1
- delays: float32 [256], P('feed'), may hold values from -64 to 64
- channel_flags: int32 [512], P('feed'), may hold values from 0 to 1, as said below
Outputs:
- visibilities: float32 [512, 256, 256], P(('feed', 'tm'))
Inputs may be any that keep to these rules, and one draw needn't show every extreme that they name: `channel_flags`: channel c belongs to owner c // 64; every owner keeps between 16 and 64 of its channels, and in every draw some owner keeps all of them.
All inputs are finite; a program needn't handle non-finite values.
Results may differ from a plain program's by a relative error of at most 0.0011.
Values may be sent and summed in bfloat16 or wider, within the bound.
A program may use at most 192 MiB of HBM per device.

v0:
```python
import math
import jax
import jax.numpy as jnp
from jax import lax
from jax.sharding import PartitionSpec as P


def passed_along(block, axis, distance):
    devices = range(lax.axis_size(axis))
    route = [(i - distance, i) for i in devices if i - distance in devices]
    return lax.ppermute(block, axis, route)


def build_table(fft_length):
    channels = jnp.arange(fft_length // 2, dtype=jnp.int32)
    samples = jnp.arange(fft_length, dtype=jnp.int32)
    product = channels[:, None] * samples[None, :] % fft_length
    angles = product.astype(jnp.float32) * (2.0 * math.pi / fft_length)
    return jnp.stack([jnp.cos(angles), -jnp.sin(angles)], axis=1).astype(jnp.bfloat16)


def rotate_phase(real_part, imag_part, channels, delay_values, fft_length):
    angles = 2.0 * math.pi / fft_length * channels * delay_values
    cosine = jnp.cos(angles)
    sine_part = jnp.sin(angles)
    factor = 1.0 / math.sqrt(fft_length)
    return (
        (real_part * cosine + imag_part * sine_part) * factor,
        (imag_part * cosine - real_part * sine_part) * factor,
    )


def gram_blocks(turned, local_frame_count, frame_total):
    count_here, inputs_all, columns = turned.shape
    split = turned.reshape(
        count_here, inputs_all, columns // (2 * local_frame_count), 2, local_frame_count
    )
    real_half = split[:, :, :, 0].reshape(count_here, inputs_all, columns // 2)
    imag_half = split[:, :, :, 1].reshape(count_here, inputs_all, columns // 2)
    block_rows = min(128, inputs_all)
    column_index = jnp.arange(inputs_all)[None, :]
    row_blocks = []
    for first in range(0, inputs_all, block_rows):
        last = first + block_rows
        upper = jnp.einsum(
            "cik,cjk->cij",
            turned[:, first:last],
            turned[:, first:],
            preferred_element_type=jnp.float32,
        )
        lower = jnp.einsum(
            "cik,cjk->cij",
            imag_half[:, first:last],
            real_half[:, :last],
            preferred_element_type=jnp.float32,
        )
        lower = lower - jnp.einsum(
            "cik,cjk->cij",
            real_half[:, first:last],
            imag_half[:, :last],
            preferred_element_type=jnp.float32,
        )
        upper_full = jnp.pad(upper, ((0, 0), (0, 0), (first, 0)))
        lower_full = jnp.pad(lower, ((0, 0), (0, 0), (0, inputs_all - last)))
        row_index = jnp.arange(first, last)[:, None]
        row_blocks.append(jnp.where(row_index <= column_index, upper_full, lower_full))
    return jnp.concatenate(row_blocks, axis=1) / frame_total


def on_device(voltages, filter_taps, delays, channel_flags):
    inputs_here, sample_count = voltages.shape
    tap_count, fft_length = filter_taps.shape
    local_frame_count = sample_count // fft_length
    frames = voltages.reshape(inputs_here, local_frame_count, fft_length)
    history = passed_along(frames[:, local_frame_count - (tap_count - 1) :, :], "tm", 1)
    extended = jnp.concatenate([history, frames], axis=1).astype(jnp.float32)
    filtered = filter_taps[0] * extended[:, tap_count - 1 : tap_count - 1 + local_frame_count]
    for tap_index in range(1, tap_count):
        offset = tap_count - 1 - tap_index
        filtered = (
            filtered + filter_taps[tap_index] * extended[:, offset : offset + local_frame_count]
        )
    filtered = filtered.astype(jnp.bfloat16)
    dft_table = build_table(fft_length)
    raw_spectra = jnp.einsum(
        "cpn,isn->cips", dft_table, filtered, preferred_element_type=jnp.float32
    )
    channels = jnp.arange(fft_length // 2).astype(jnp.float32)[:, None, None]
    real_part, imag_part = rotate_phase(
        raw_spectra[:, :, 0], raw_spectra[:, :, 1], channels, delays[None, :, None], fft_length
    )
    spectra = jnp.concatenate([real_part, imag_part], axis=2).astype(jnp.bfloat16)
    time_devices = lax.axis_size("tm")
    frame_total = local_frame_count * time_devices
    channels_here = channel_flags.shape[0] // time_devices
    local_flags = lax.dynamic_slice_in_dim(
        channel_flags, lax.axis_index("tm") * channels_here, channels_here, 0
    )
    turned = lax.all_to_all(spectra, "feed", split_axis=0, concat_axis=1, tiled=True)
    visibility = lax.psum_scatter(
        gram_blocks(turned, local_frame_count, frame_total), "tm", scatter_dimension=0, tiled=True
    )
    return visibility * local_flags[:, None, None].astype(jnp.float32)


def solution(mesh):
    in_specs = (P("feed", "tm"), P(), P("feed"), P("feed"))
    out_specs = P(("feed", "tm"), None, None)
    return jax.shard_map(
        on_device, mesh=mesh, in_specs=in_specs, out_specs=out_specs, check_vma=False
    )
```

profile of v0, /device:TPU:0, one launch (start us, length us, event | category | flops | bytes accessed | tf_op | source)
XLA Modules:
  0.0 797.1 jit_solution(467650899731393742)
XLA Ops:
  6.5 15.4 %copy.23 = bf16[4,8,256,1024]{3,2,1,0:T(8,128)(2,1)S(1)} copy(bf16[4,8,256,1024]{3,1,2,0:T(8,128)(2,1)} %bitcast.67) | data formatting | bytes 33554432
  21.9 0.1 slice.79
  22.1 4.9 collective-permute-start
  27.0 8.5 %negate_convert_fusion = (bf16[512,1,1024]{2,0,1:T(8,128)(2,1)S(1)}, bf16[512,1,1024]{2,0,1:T(8,128)(2,1)S(1)}) fusion(), kind=kLoop, calls=%fused_computation.49 | loop fusion | flops 8912896 | bytes 2097152 | tf_op jit(solution)/shard_map/convert.3
  35.6 0.3 multiply_cosine_fusion
  35.9 12.0 %maximum_convert_fusion = f32[32,259,1024]{2,1,0:T(8,128)} fusion(bf16[32,256,1024]{2,1,0:T(8,128)(2,1)S(1)} %bitcast.66, bf16[32,3,1024]{2,1,0:T(4,128)(2,1)S(1)} %collective-permute-done), kind=kLoop, calls=%fused_computation.8 | loop fusion | flops 33947648 | bytes 50921472 | tf_op jit(solution)/shard_map/convert_element_type | solution.py:76
  47.9 56.9 %fusion.10 = f32[512,32,2,256]{0,3,2,1:T(8,128)} fusion(f32[32,259,1024]{2,1,0:T(8,128)} %maximum_convert_fusion, f32[1024]{0:T(1024)S(1)} %bitcast.70, f32[1024]{0:T(1024)S(1)} %bitcast.71, f32[1024]{0:T(1024)S(1)} %bitcast.69, f32[1024]{0:T(1024)S(1)} %bitcast.68, bf16[512,1,1024]{2,0,1:T(8,128)(2,1)S(1)} %get-tuple-element.15, ...), kind=kOutput, calls=%fused_computation.20 | convolution fusion | flops 17251172352 | bytes 169885696 | tf_op jit(solution)/shard_map/cpn,isn->cips/dot_general | solution.py:85
  104.8 12.3 %multiply_convert_fusion.1 = (bf16[512,32,256]{0,2,1:T(8,128)(2,1)S(1)}, bf16[512,32,256]{0,2,1:T(8,128)(2,1)S(1)}) fusion(f32[512,32,2,256]{0,3,2,1:T(8,128)} %fusion.10, f32[512,32]{0,1:T(8,128)S(1)} %get-tuple-element.14, f32[512,32]{0,1:T(8,128)S(1)} %get-tuple-element.13), kind=kLoop, calls=%fused_computation.16 | loop fusion | flops 41943040 | bytes 50462720 | tf_op jit(solution)/shard_map/convert
  117.1 6.5 pad_maximum_fusion
  123.6 28.6 %copy.14 = bf16[512,32,512]{2,1,0:T(8,128)(2,1)} copy(bf16[512,32,512]{0,2,1:T(8,128)(2,1)} %pad_maximum_fusion) | data formatting | bytes 33554432 | tf_op jit(solution)/shard_map/concatenate | solution.py:92
  152.3 5.7 all-to-all-start
  158.0 0.2 reduce-scatter.2.cloned.1.call-start
  158.3 0.1 iota_compare_fusion
  158.4 183.6 %all-to-all-done = bf16[512,32,512]{2,1,0:T(8,128)(2,1)} async-done(((bf16[512,32,512]{2,1,0:T(8,128)(2,1)}), bf16[512,32,512]{2,1,0:T(8,128)(2,1)}, u32[]{:S(2)}, u32[]{:S(2)}) %all-to-all-start) | async-done | bytes 16777248 | tf_op jit(solution)/shard_map/all_to_all | solution.py:99
  341.9 14.1 %copy.15 = bf16[64,8,32,512]{3,2,1,0:T(8,128)(2,1)} copy(bf16[64,8,32,512]{3,2,0,1:T(8,128)(2,1)} %bitcast.11) | data formatting | bytes 33554432 | tf_op jit(solution)/shard_map/all_to_all | solution.py:99
  356.0 23.7 %reshape.151 = bf16[64,256,1,2,256]{4,3,1,0,2:T(2,128)(2,1)} reshape(bf16[64,8,32,512]{3,2,1,0:T(8,128)(2,1)} %copy.15) | data formatting | bytes 33554432 | tf_op jit(solution)/shard_map/reshape | solution.py:35
  379.7 32.4 %fusion.45 = (bf16[64,256,1,1,256]{4,3,1,0,2:T(2,128)(2,1)}, bf16[64,256,1,1,256]{4,3,1,0,2:T(2,128)(2,1)}) fusion(bf16[64,256,1,2,256]{4,3,1,0,2:T(2,128)(2,1)} %reshape.151), kind=kLoop, calls=%fused_computation.63 | loop fusion | bytes 33554432 | tf_op jit(solution)/shard_map/slice | solution.py:38
  412.2 8.9 %copy.26 = bf16[64,256,1,1,256]{4,1,0,3,2:T(8,128)(2,1)S(1)} copy(bf16[64,256,1,1,256]{4,3,1,0,2:T(2,128)(2,1)} %get-tuple-element.7) | data formatting | bytes 16777216
  421.1 11.9 %copy.27 = bf16[64,256,1,1,256]{4,1,0,3,2:T(8,128)(2,1)S(1)} copy(bf16[64,256,1,1,256]{4,3,1,0,2:T(2,128)(2,1)} %get-tuple-element.8) | data formatting | bytes 16777216
  433.1 3.2 copy-done.1
  436.3 3.3 fusion.21
  439.6 9.5 %fusion.17 = f32[64,128,256]{2,1,0:T(8,128)} fusion(bf16[64,256,256]{2,1,0:T(8,128)(2,1)} %bitcast.62, bf16[64,256,256]{2,1,0:T(8,128)(2,1)S(1)} %bitcast.58), kind=kOutput, calls=%fused_computation.29 | convolution fusion | flops 1073741824 | bytes 20971520 | tf_op jit(solution)/shard_map/cik,cjk->cij/dot_general | solution.py:57
  449.0 6.8 fusion.37
  455.9 10.1 %fusion.13 = f32[64,128,128]{2,1,0:T(8,128)} fusion(bf16[64,256,512]{2,1,0:T(8,128)(2,1)} %bitcast.55), kind=kOutput, calls=%fused_computation.21 | convolution fusion | flops 1073741824 | bytes 12582912 | tf_op jit(solution)/shard_map/cik,cjk->cij/dot_general | solution.py:45
  466.0 15.0 %pad_select_fusion = f32[64,128,256]{2,1,0:T(8,128)} fusion(f32[64,128,128]{2,1,0:T(8,128)} %fusion.37, pred[128,256]{1,0:T(8,128)(4,1)S(1)} %iota_compare_fusion.1, bf16[64,256,512]{2,1,0:T(8,128)(2,1)} %bitcast.56), kind=kOutput, calls=%fused_computation.28 | convolution fusion | flops 2149580800 | bytes 37781504 | tf_op jit(solution)/shard_map/cik,cjk->cij/dot_general | solution.py:45
  481.0 14.2 %subtract_select_fusion = f32[64,128,256]{2,1,0:T(8,128)} fusion(f32[64,128,256]{2,1,0:T(8,128)} %fusion.17, f32[64,128,128]{2,1,0:T(8,128)} %fusion.13, pred[128,256]{1,0:T(8,128)(4,1)S(1)} %iota_compare_fusion, bf16[64,256,256]{2,1,0:T(8,128)(2,1)} %bitcast.60, bf16[64,256,256]{2,1,0:T(8,128)(2,1)} %bitcast.64), kind=kOutput, calls=%fused_computation.27 | convolution fusion | flops 1077936128 | bytes 33587200 | tf_op jit(solution)/shard_map/cik,cjk->cij/dot_general | solution.py:51
  495.2 11.4 %maximum_multiply_fusion = f32[64,256,256]{2,1,0:T(8,128)} fusion(f32[64,128,256]{2,1,0:T(8,128)} %subtract_select_fusion, f32[64,128,256]{2,1,0:T(8,128)} %pad_select_fusion), kind=kLoop, calls=%fused_computation.12 | loop fusion | flops 8388608 | bytes 33554432 | tf_op jit(solution)/shard_map/div | solution.py:67
  506.7 0.0 reduce-scatter.2.cloned.1.call-update
  506.7 0.6 copy-done.4
  507.3 0.1 dynamic-slice_convert_fusion
  507.4 278.1 %reduce-scatter.2.cloned.1.call-done = f32[16,256,256]{2,1,0:T(8,128)} async-done(((f32[64,256,256]{2,1,0:T(8,128)}), f32[16,256,256]{2,1,0:T(8,128)}) %reduce-scatter.2.cloned.1.call-update) | async-done | bytes 4194320 | tf_op jit(solution)/shard_map/reduce_scatter | solution.py:100
  785.5 4.7 broadcast_multiply_fusion
  (13 shorter events, 0.1 us)
Async XLA Ops:
  6.5 29.0 %copy-start.3 = (f32[32]{0:T(128)S(1)}, f32[32]{0:T(128)}, u32[]{:S(2)}) copy-start(f32[32]{0:T(128)} %param.6) | copy-start | bytes 388
  6.5 29.3 %copy-start.2 = (f32[4,1024]{1,0:T(4,128)S(1)}, f32[4,1024]{1,0:T(4,128)}, u32[]{:S(2)}) copy-start(f32[4,1024]{1,0:T(4,128)} %param.5) | copy-start | bytes 49156
  22.1 13.8 %collective-permute-start = (bf16[32,3,1024]{2,1,0:T(4,128)(2,1)S(1)}, bf16[32,3,1024]{2,1,0:T(4,128)(2,1)S(1)}, u32[]{:S(2)}, u32[]{:S(2)}) collective-permute-start(bf16[32,3,1024]{2,1,0:T(4,128)(2,1)S(1)} %slice.79), channel_id=1, source_target_pairs={{0,1},{1,2},{2,3},{4,5},{5,6},{6,7},{8,9},{9,10},{10,11},{12,13},{... | collective-permute-start | bytes 589832 | tf_op jit(solution)/shard_map/ppermute | solution.py:11
  152.3 189.7 %all-to-all-start = ((bf16[512,32,512]{2,1,0:T(8,128)(2,1)}), bf16[512,32,512]{2,1,0:T(8,128)(2,1)}, u32[]{:S(2)}, u32[]{:S(2)}) async-start(bf16[512,32,512]{2,1,0:T(8,128)(2,1)} %copy.14), calls=%async_computation | async-start | bytes 33554432 | tf_op jit(solution)/shard_map/all_to_all | solution.py:99
  158.0 627.5 %reduce-scatter.2.cloned.1.call-start = ((), (), s32[]{:S(2)}) async-start(), calls=%async_computation.2 | async-start | bytes 20971520 | tf_op jit(solution)/shard_map/reduce_scatter | solution.py:100
  421.1 28.0 %copy-start = (bf16[64,256,1,1,256]{4,1,0,3,2:T(8,128)(2,1)}, bf16[64,256,1,1,256]{4,1,0,3,2:T(8,128)(2,1)S(1)}, u32[]{:S(2)}) copy-start(bf16[64,256,1,1,256]{4,1,0,3,2:T(8,128)(2,1)S(1)} %copy.26) | copy-start | bytes 25165828
  433.1 3.2 copy-start.1
  506.7 0.7 copy-start.4
Sparse Core Ops, SparseCore 0:
  506.8 278.6 reduce-scatter.1
where the time goes:
time: 799 us; the launch traced here: 797 us
  waiting for transfers between devices  462 us (58%)
  local copies, waits for them, and re-layouts  139 us (17%)
  matrix products  116 us (15%)
  other arithmetic  55.9 us (7%)
  between operations  13.6 us (2%)
  starting transfers between devices  10.9 us (1%)
    reduce_scatter x1, waiting for transfers between devices, on_device(): lax.psum_scatter(gram_blocks(turned, local_frame_count, frame_total), 'tm...  278 us
    all_to_all x1, waiting for transfers between devices, on_device(): lax.all_to_all(spectra, 'feed', split_axis=0, concat_axis=1, tiled=True)  184 us
    dot_general x1, matrix products, on_device(): jnp.einsum('cpn,isn->cips', dft_table, filtered, preferred_element_type=j...  56.9 us
    unnamed x13, local copies, waits for them, and re-layouts  40.1 us
    slice x1, local copies, waits for them, and re-layouts, gram_blocks(): real_half = split[:, :, :, 0].reshape(count_here, inputs_all, columns // 2)  32.4 us
    concatenate x1, local copies, waits for them, and re-layouts, on_device(): jnp.concatenate([real_part, imag_part], axis=2).astype(jnp.bfloat16)  28.6 us
    dot_general x2, matrix products, gram_blocks(): jnp.einsum('cik,cjk->cij', turned[:, first:last], turned[:, first:], pref...  25.1 us
    reshape x1, local copies, waits for them, and re-layouts, gram_blocks(): turned.reshape(count_here, inputs_all, columns // (2 * local_frame_count)...  23.7 us
  transfers between devices with their start and end apart: 3, of which 2 were waited for; matrix products, arithmetic and copies ran while one was open for 1% of the time, Pallas kernels for 0%

commit v1 on v0

--- a/solution.py
+++ b/solution.py
@@ -96,7 +96,25 @@
     local_flags = lax.dynamic_slice_in_dim(
         channel_flags, lax.axis_index("tm") * channels_here, channels_here, 0
     )
-    turned = lax.all_to_all(spectra, "feed", split_axis=0, concat_axis=1, tiled=True)
+    later, formed = (jax.lax.axis_size("feed"), jax.lax.axis_index("feed"))
+    block_now = spectra.shape[0] // later
+    y1 = list(spectra.shape)
+    y1[0] = block_now
+    m_next = y1[1]
+    y1[1] = m_next * later
+    turned = jnp.zeros(y1, spectra.dtype)
+    c = 0
+    while c < later:
+        new = lax.dynamic_slice_in_dim(spectra, (formed ^ c) * block_now, block_now, axis=0)
+        if c:
+            kept_rows = []
+            src_i = 0
+            while src_i < later:
+                kept_rows.append((src_i, src_i ^ c))
+                src_i += 1
+            new = jax.lax.ppermute(new, "feed", perm=kept_rows)
+        turned = lax.dynamic_update_slice_in_dim(turned, new, (formed ^ c) * m_next, axis=1)
+        c += 1
     visibility = lax.psum_scatter(
         gram_blocks(turned, local_frame_count, frame_total), "tm", scatter_dimension=0, tiled=True
     )

time: 799 us -> 816 us (1.021); the launches traced: 797 us -> 804 us
  waiting for transfers between devices: 462 us -> 408 us
  local copies, waits for them, and re-layouts: 139 us -> 175 us
  other arithmetic: 55.9 us -> 78.3 us
    all_to_all x1 -> x0, waiting for transfers between devices: 184 us -> none  [on_device(): lax.all_to_all(spectra, 'feed', split_axis=0, concat_axis=1, tiled=True)]
    ppermute x0 -> x7, waiting for transfers between devices: none -> 127 us  [on_device(): new = jax.lax.ppermute(new, 'feed', perm=kept_rows)]
    dynamic_slice x0 -> x8, local copies, waits for them, and re-layouts: none -> 43.6 us  [on_device(): lax.dynamic_slice_in_dim(spectra, (formed ^ c) * block_now, block_now, ax...]
    concatenate x1 -> x0, local copies, waits for them, and re-layouts: 28.6 us -> none  [on_device(): jnp.concatenate([real_part, imag_part], axis=2).astype(jnp.bfloat16)]
    dynamic_update_slice x0 -> x8, local copies, waits for them, and re-layouts: none -> 23.2 us  [on_device(): lax.dynamic_update_slice_in_dim(turned, new, (formed ^ c) * m_next, axis=1)]
    concatenate x1 -> x2, other arithmetic: 6.52 us -> 21.8 us  [on_device(): jnp.concatenate([real_part, imag_part], axis=2).astype(jnp.bfloat16)]
    all_to_all x1 -> x0, local copies, waits for them, and re-layouts: 14.1 us -> none  [on_device(): lax.all_to_all(spectra, 'feed', split_axis=0, concat_axis=1, tiled=True)]
    unnamed x13 -> x19, local copies, waits for them, and re-layouts: 40.1 us -> 46 us
  transfers between devices with their start and end apart: 3 -> 9, of which waited for: 2 -> 4; matrix products, arithmetic and copies ran while one was open for 1% -> 10% of each run, Pallas kernels for 0% -> 0%
where the time goes in v1:
time: 816 us; the launch traced here: 804 us
  waiting for transfers between devices  408 us (50%)
  local copies, waits for them, and re-layouts  175 us (21%)
  matrix products  117 us (14%)
  other arithmetic  78.3 us (10%)
  between operations  14 us (2%)
  starting transfers between devices  12.4 us (2%)
    reduce_scatter x1, waiting for transfers between devices, on_device(): lax.psum_scatter(gram_blocks(turned, local_frame_count, frame_total), 'tm...  280 us
    ppermute x7, waiting for transfers between devices, on_device(): new = jax.lax.ppermute(new, 'feed', perm=kept_rows)  127 us
    dot_general x1, matrix products, on_device(): jnp.einsum('cpn,isn->cips', dft_table, filtered, preferred_element_type=j...  56.7 us
    unnamed x19, local copies, waits for them, and re-layouts  46 us
    dynamic_slice x8, local copies, waits for them, and re-layouts, on_device(): lax.dynamic_slice_in_dim(spectra, (formed ^ c) * block_now, block_now, ax...  43.6 us
    slice x1, local copies, waits for them, and re-layouts, gram_blocks(): real_half = split[:, :, :, 0].reshape(count_here, inputs_all, columns // 2)  32.4 us
    dot_general x2, matrix products, gram_blocks(): jnp.einsum('cik,cjk->cij', turned[:, first:last], turned[:, first:], pref...  25.2 us
    reshape x1, local copies, waits for them, and re-layouts, gram_blocks(): turned.reshape(count_here, inputs_all, columns // (2 * local_frame_count)...  23.8 us
  transfers between devices with their start and end apart: 9, of which 4 were waited for; matrix products, arithmetic and copies ran while one was open for 10% of the time, Pallas kernels for 0%

profile of v1, /device:TPU:0, one launch (start us, length us, event | category | flops | bytes accessed | tf_op | source)
XLA Modules:
  0.0 804.1 jit_solution(2741663918819949896)
XLA Ops:
  6.5 15.4 %copy.31 = bf16[4,8,256,1024]{3,2,1,0:T(8,128)(2,1)S(1)} copy(bf16[4,8,256,1024]{3,1,2,0:T(8,128)(2,1)} %bitcast.59) | data formatting | bytes 33554432
  22.0 5.8 copy-done.4
  27.9 4.9 collective-permute-start
  32.9 8.5 %negate_convert_fusion = (bf16[512,1,1024]{2,0,1:T(8,128)(2,1)S(1)}, bf16[512,1,1024]{2,0,1:T(8,128)(2,1)S(1)}) fusion(), kind=kLoop, calls=%fused_computation.72 | loop fusion | flops 8912896 | bytes 2097152 | tf_op jit(solution)/shard_map/convert.3
  41.8 19.1 %maximum_convert_fusion = f32[32,259,1024]{2,1,0:T(8,128)} fusion(bf16[32,256,1024]{2,1,0:T(8,128)(2,1)} %bitcast.58, bf16[32,3,1024]{2,1,0:T(4,128)(2,1)S(1)} %collective-permute-done), kind=kLoop, calls=%fused_computation.24 | loop fusion | flops 33947648 | bytes 50921472 | tf_op jit(solution)/shard_map/convert_element_type | solution.py:76
  60.9 56.7 %fusion.10 = f32[512,32,2,256]{0,3,2,1:T(8,128)} fusion(f32[32,259,1024]{2,1,0:T(8,128)} %maximum_convert_fusion, f32[1024]{0:T(1024)S(1)} %bitcast.62, f32[1024]{0:T(1024)S(1)} %bitcast.63, f32[1024]{0:T(1024)S(1)} %bitcast.61, f32[1024]{0:T(1024)S(1)} %bitcast.60, bf16[512,1,1024]{2,0,1:T(8,128)(2,1)S(1)} %get-tuple-element.23, ...), kind=kOutput, calls=%fused_computation.35 | convolution fusion | flops 17251172352 | bytes 169885696 | tf_op jit(solution)/shard_map/cpn,isn->cips/dot_general | solution.py:85
  117.6 12.3 %multiply_convert_fusion = (bf16[512,32,256]{0,2,1:T(8,128)(2,1)S(1)}, bf16[512,32,256]{0,2,1:T(8,128)(2,1)S(1)}) fusion(f32[512,32,2,256]{0,3,2,1:T(8,128)} %fusion.10, f32[512,32]{0,1:T(8,128)S(1)} %get-tuple-element.22, f32[512,32]{0,1:T(8,128)S(1)} %get-tuple-element.21), kind=kLoop, calls=%fused_computation.30 | loop fusion | flops 41943040 | bytes 50462720 | tf_op jit(solution)/shard_map/convert.1
  129.9 14.0 %fusion.17 = (bf16[64,32,512]{0,2,1:T(8,128)(2,1)}, bf16[64,32,512]{0,2,1:T(8,128)(2,1)}, bf16[64,32,512]{0,2,1:T(8,128)(2,1)}, bf16[64,32,512]{0,2,1:T(8,128)(2...) fusion(s32[]{:T(128)S(6)} %select_n.93, bf16[512,32,256]{0,2,1:T(8,128)(2,1)S(1)} %get-tuple-element.6, ...), kind=kLoop, calls=%fused_computation.44 | loop fusion | flops 25165824 | bytes 29360152 | tf_op jit(solution)/shard_map/concatenate | solution.py:92
  144.0 5.7 copy.18
  155.9 5.7 copy.20
  161.9 5.8 copy.21
  169.3 7.8 fusion.24
  177.1 5.7 copy.22
  182.8 5.7 copy.23
  191.0 5.7 copy.24
  196.7 6.2 collective-permute-done.2
  204.5 4.7 copy.17
  209.1 5.9 broadcast_in_dim.10
  222.7 24.4 %collective-permute-done.3 = bf16[64,32,512]{2,1,0:T(8,128)(2,1)} collective-permute-done((bf16[64,32,512]{2,1,0:T(8,128)(2,1)}, bf16[64,32,512]{2,1,0:T(8,128)(2,1)}, u32[]{:S(2)}, u32[]{:S(2)}) %collective-permute-start.3) | collective-permute-done | bytes 2097184 | tf_op jit(solution)/shard_map/ppermute | solution.py:115
  253.3 96.7 %collective-permute-done.5 = bf16[64,32,512]{2,1,0:T(8,128)(2,1)} collective-permute-done((bf16[64,32,512]{2,1,0:T(8,128)(2,1)}, bf16[64,32,512]{2,1,0:T(8,128)(2,1)}, u32[]{:S(2)}, u32[]{:S(2)}) %collective-permute-start.5) | collective-permute-done | bytes 2097184 | tf_op jit(solution)/shard_map/ppermute | solution.py:115
  359.4 23.8 %reshape.150 = bf16[64,256,1,2,256]{4,3,1,0,2:T(2,128)(2,1)} reshape(bf16[64,256,512]{2,1,0:T(8,128)(2,1)} %constant_dynamic-update-slice_fusion) | data formatting | bytes 33554432 | tf_op jit(solution)/shard_map/reshape | solution.py:35
  383.2 32.4 %fusion.53 = (bf16[64,256,1,1,256]{4,3,1,0,2:T(2,128)(2,1)}, bf16[64,256,1,1,256]{4,3,1,0,2:T(2,128)(2,1)}) fusion(bf16[64,256,1,2,256]{4,3,1,0,2:T(2,128)(2,1)} %reshape.150), kind=kLoop, calls=%fused_computation.94 | loop fusion | bytes 33554432 | tf_op jit(solution)/shard_map/slice | solution.py:38
  415.6 8.9 %copy.34 = bf16[64,256,1,1,256]{4,1,0,3,2:T(8,128)(2,1)S(1)} copy(bf16[64,256,1,1,256]{4,3,1,0,2:T(2,128)(2,1)} %get-tuple-element.7) | data formatting | bytes 16777216
  424.6 11.9 %copy.35 = bf16[64,256,1,1,256]{4,1,0,3,2:T(8,128)(2,1)S(1)} copy(bf16[64,256,1,1,256]{4,3,1,0,2:T(2,128)(2,1)} %get-tuple-element.8) | data formatting | bytes 16777216
  443.0 9.5 %fusion.25 = f32[64,128,256]{2,1,0:T(8,128)} fusion(bf16[64,256,256]{2,1,0:T(8,128)(2,1)} %bitcast.54, bf16[64,256,256]{2,1,0:T(8,128)(2,1)S(1)} %bitcast.50), kind=kOutput, calls=%fused_computation.52 | convolution fusion | flops 1073741824 | bytes 20971520 | tf_op jit(solution)/shard_map/cik,cjk->cij/dot_general | solution.py:57
  452.5 10.1 %fusion.13 = f32[64,128,128]{2,1,0:T(8,128)} fusion(bf16[64,256,512]{2,1,0:T(8,128)(2,1)} %constant_dynamic-update-slice_fusion), kind=kOutput, calls=%fused_computation.36 | convolution fusion | flops 1073741824 | bytes 12582912 | tf_op jit(solution)/shard_map/cik,cjk->cij/dot_general | solution.py:45
  462.7 7.9 fusion.45
  470.6 15.0 %pad_select_fusion = f32[64,128,256]{2,1,0:T(8,128)} fusion(f32[64,128,128]{2,1,0:T(8,128)} %fusion.45, pred[128,256]{1,0:T(8,128)(4,1)S(1)} %iota_compare_fusion.1, bf16[64,256,512]{2,1,0:T(8,128)(2,1)} %constant_dynamic-update-slice_fusion), kind=kOutput, calls=%fused_computation.43 | convolution fusion | flops 2149580800 | bytes 37781504 | tf_op jit(solution)/shard_map/cik,cjk->cij/dot_general | solution.py:45
  485.6 14.3 %subtract_select_fusion = f32[64,128,256]{2,1,0:T(8,128)} fusion(f32[64,128,256]{2,1,0:T(8,128)} %fusion.25, f32[64,128,128]{2,1,0:T(8,128)} %fusion.13, pred[128,256]{1,0:T(8,128)(4,1)S(1)} %iota_compare_fusion, bf16[64,256,256]{2,1,0:T(8,128)(2,1)} %bitcast.52, bf16[64,256,256]{2,1,0:T(8,128)(2,1)} %bitcast.56), kind=kOutput, calls=%fused_computation.42 | convolution fusion | flops 1077936128 | bytes 33587200 | tf_op jit(solution)/shard_map/cik,cjk->cij/dot_general | solution.py:51
  499.8 11.4 %maximum_multiply_fusion = f32[64,256,256]{2,1,0:T(8,128)} fusion(f32[64,128,256]{2,1,0:T(8,128)} %subtract_select_fusion, f32[64,128,256]{2,1,0:T(8,128)} %pad_select_fusion), kind=kLoop, calls=%fused_computation.27 | loop fusion | flops 8388608 | bytes 33554432 | tf_op jit(solution)/shard_map/div | solution.py:67
  512.0 280.1 %reduce-scatter.2.cloned.1.call-done = f32[16,256,256]{2,1,0:T(8,128)} async-done(((f32[64,256,256]{2,1,0:T(8,128)}), f32[16,256,256]{2,1,0:T(8,128)}) %reduce-scatter.2.cloned.1.call-update) | async-done | bytes 4194320 | tf_op jit(solution)/shard_map/reduce_scatter | solution.py:118
  792.2 4.7 broadcast_multiply_fusion
  (47 shorter events, 43.2 us)
Async XLA Ops:
  6.5 785.6 %reduce-scatter.2.cloned.1.call-start = ((), (), s32[]{:S(2)}) async-start(), calls=%async_computation.1 | async-start | bytes 20971520 | tf_op jit(solution)/shard_map/reduce_scatter | solution.py:118
  6.5 34.9 %copy-start.6 = (f32[32]{0:T(128)S(1)}, f32[32]{0:T(128)}, u32[]{:S(2)}) copy-start(f32[32]{0:T(128)} %param.6) | copy-start | bytes 388
  6.5 35.2 %copy-start.5 = (f32[4,1024]{1,0:T(4,128)S(1)}, f32[4,1024]{1,0:T(4,128)}, u32[]{:S(2)}) copy-start(f32[4,1024]{1,0:T(4,128)} %param.5) | copy-start | bytes 49156
  21.9 5.8 copy-start.4
  27.9 13.9 %collective-permute-start = (bf16[32,3,1024]{2,1,0:T(4,128)(2,1)S(1)}, bf16[32,3,1024]{2,1,0:T(4,128)(2,1)S(1)}, u32[]{:S(2)}, u32[]{:S(2)}) collective-permute-start(bf16[32,3,1024]{2,1,0:T(4,128)(2,1)S(1)} %slice.79), channel_id=1, source_target_pairs={{0,1},{1,2},{2,3},{4,5},{5,6},{6,7},{8,9},{9,10},{10,11},{12,13},{... | collective-permute-start | bytes 589832 | tf_op jit(solution)/shard_map/ppermute | solution.py:11
  129.9 14.0 %copy-start.2 = (bf16[512,32,256]{0,2,1:T(8,128)(2,1)}, bf16[512,32,256]{0,2,1:T(8,128)(2,1)S(1)}, u32[]{:S(2)}) copy-start(bf16[512,32,256]{0,2,1:T(8,128)(2,1)S(1)} %get-tuple-element.5) | copy-start | bytes 25165828
  129.9 14.0 %copy-start.3 = (bf16[512,32,256]{0,2,1:T(8,128)(2,1)}, bf16[512,32,256]{0,2,1:T(8,128)(2,1)S(1)}, u32[]{:S(2)}) copy-start(bf16[512,32,256]{0,2,1:T(8,128)(2,1)S(1)} %get-tuple-element.6) | copy-start | bytes 25165828
  149.6 38.9 %collective-permute-start.1 = (bf16[64,32,512]{2,1,0:T(8,128)(2,1)}, bf16[64,32,512]{2,1,0:T(8,128)(2,1)}, u32[]{:S(2)}, u32[]{:S(2)}) collective-permute-start(bf16[64,32,512]{2,1,0:T(8,128)(2,1)} %copy.18), channel_id=1, source_target_pairs={{0,4},{4,0},{8,12},{12,8},{16,20},{20,16},{24,28},{28,24},{1,5},{5... | collective-permute-start | bytes 6291464 | tf_op jit(solution)/shard_map/ppermute | solution.py:115
  154.3 48.6 %collective-permute-start.2 = (bf16[64,32,512]{2,1,0:T(8,128)(2,1)S(1)}, bf16[64,32,512]{2,1,0:T(8,128)(2,1)}, u32[]{:S(2)}, u32[]{:S(2)}) collective-permute-start(bf16[64,32,512]{2,1,0:T(8,128)(2,1)S(1)} %copy.19), channel_id=1, source_target_pairs={{0,8},{4,12},{8,0},{12,4},{16,24},{20,28},{24,16},{28,20},{1,9},{5... | collective-permute-start | bytes 6291464 | tf_op jit(solution)/shard_map/ppermute | solution.py:115
  161.6 85.5 %collective-permute-start.3 = (bf16[64,32,512]{2,1,0:T(8,128)(2,1)}, bf16[64,32,512]{2,1,0:T(8,128)(2,1)}, u32[]{:S(2)}, u32[]{:S(2)}) collective-permute-start(bf16[64,32,512]{2,1,0:T(8,128)(2,1)} %copy.20), channel_id=1, source_target_pairs={{0,12},{4,8},{8,4},{12,0},{16,28},{20,24},{24,20},{28,16},{1,13},{... | collective-permute-start | bytes 6291464 | tf_op jit(solution)/shard_map/ppermute | solution.py:115
  167.7 82.4 %collective-permute-start.4 = (bf16[64,32,512]{2,1,0:T(8,128)(2,1)}, bf16[64,32,512]{2,1,0:T(8,128)(2,1)}, u32[]{:S(2)}, u32[]{:S(2)}) collective-permute-start(bf16[64,32,512]{2,1,0:T(8,128)(2,1)} %copy.21), channel_id=1, source_target_pairs={{0,16},{4,20},{8,24},{12,28},{16,0},{20,4},{24,8},{28,12},{1,17},{... | collective-permute-start | bytes 6291464 | tf_op jit(solution)/shard_map/ppermute | solution.py:115
  182.7 167.3 %collective-permute-start.5 = (bf16[64,32,512]{2,1,0:T(8,128)(2,1)}, bf16[64,32,512]{2,1,0:T(8,128)(2,1)}, u32[]{:S(2)}, u32[]{:S(2)}) collective-permute-start(bf16[64,32,512]{2,1,0:T(8,128)(2,1)} %copy.22), channel_id=1, source_target_pairs={{0,20},{4,16},{8,28},{12,24},{16,4},{20,0},{24,12},{28,8},{1,21},{... | collective-permute-start | bytes 6291464 | tf_op jit(solution)/shard_map/ppermute | solution.py:115
  188.5 164.7 %collective-permute-start.6 = (bf16[64,32,512]{2,1,0:T(8,128)(2,1)}, bf16[64,32,512]{2,1,0:T(8,128)(2,1)}, u32[]{:S(2)}, u32[]{:S(2)}) collective-permute-start(bf16[64,32,512]{2,1,0:T(8,128)(2,1)} %copy.23), channel_id=1, source_target_pairs={{0,24},{4,28},{8,16},{12,20},{16,8},{20,12},{24,0},{28,4},{1,25},{... | collective-permute-start | bytes 6291464 | tf_op jit(solution)/shard_map/ppermute | solution.py:115
  202.9 153.4 %collective-permute-start.7 = (bf16[64,32,512]{2,1,0:T(8,128)(2,1)}, bf16[64,32,512]{2,1,0:T(8,128)(2,1)}, u32[]{:S(2)}, u32[]{:S(2)}) collective-permute-start(bf16[64,32,512]{2,1,0:T(8,128)(2,1)} %copy.24), channel_id=1, source_target_pairs={{0,28},{4,24},{8,20},{12,16},{16,12},{20,8},{24,4},{28,0},{1,29},{... | collective-permute-start | bytes 6291464 | tf_op jit(solution)/shard_map/ppermute | solution.py:115
  424.6 18.4 %copy-start = (bf16[64,256,1,1,256]{4,1,0,3,2:T(8,128)(2,1)}, bf16[64,256,1,1,256]{4,1,0,3,2:T(8,128)(2,1)S(1)}, u32[]{:S(2)}) copy-start(bf16[64,256,1,1,256]{4,1,0,3,2:T(8,128)(2,1)S(1)} %copy.34) | copy-start | bytes 25165828
  436.5 3.3 copy-start.1
  511.3 0.7 copy-start.7
Sparse Core Ops, SparseCore 0:
  511.4 280.6 reduce-scatter.1
